TPU v7x, 32 devices: a whole 2x2x4 slice. The times are simulated.
32 devices in a mesh: ctx: 16 (over z, y, core), wsh: 2 (over x).
Axes of the slice: x: 2, y: 2, z: 4, core: 2. Of those that a mesh axis runs over, the one named last changes fastest.
Arguments:
- tokens: bfloat16 [2, 4096, 1472], P('wsh', 'ctx'), may hold values from -6 to 6
- lengths: int32 [2, 1], P('wsh'), may hold values from 1024 to 4096, as said below
- buckets: int32 [255], replicated, may hold values from 0 to 31, as said below
- attention_gain: bfloat16 [1472], P('wsh'), may hold values from 0.5 to 1.5
- query_weight: bfloat16 [1472, 384], P('wsh'), may hold values from -0.078125 to 0.078125
- key_weight: bfloat16 [1472, 384], P('wsh'), may hold values from -0.078125 to 0.078125
- value_weight: bfloat16 [1472, 384], P('wsh'), may hold values from -0.15625 to 0.15625
- output_weight: bfloat16 [384, 1472], P(None, 'wsh'), may hold values from -2.5 to 2.5
- bias_table: bfloat16 [32, 6], P('wsh'), may hold values from -3 to 3
- feed_gain: bfloat16 [1472], P('wsh'), may hold values from 0.5 to 1.5
- gate_weight: bfloat16 [1472, 3584], P(None, 'wsh'), may hold values from -0.15625 to 0.15625
- up_weight: bfloat16 [1472, 3584], P(None, 'wsh'), may hold values from -0.15625 to 0.15625
- down_weight: bfloat16 [3584, 1472], P('wsh'), may hold values from -0.09375 to 0.09375
- cotangent: bfloat16 [2, 4096, 1472], P('wsh', 'ctx'), may hold values from -6 to 6
Outputs:
- result: bfloat16 [2, 4096, 1472], P('wsh', 'ctx')
- input_gradient: bfloat16 [2, 4096, 1472], P('wsh', 'ctx')
- attention_gain_gradient: float32 [1472], P('wsh')
- query_gradient: float32 [1472, 384], P('wsh', 'ctx')
- key_gradient: float32 [1472, 384], P('wsh', 'ctx')
- value_gradient: float32 [1472, 384], P('wsh', 'ctx')
- output_gradient: float32 [384, 1472], P('ctx', 'wsh')
- bias_gradient: float32 [32, 6], P('wsh')
- feed_gain_gradient: float32 [1472], P('wsh')
- gate_gradient: float32 [1472, 3584], P(None, ('ctx', 'wsh'))
- up_gradient: float32 [1472, 3584], P(None, ('ctx', 'wsh'))
- down_gradient: float32 [3584, 1472], P(('ctx', 'wsh'))
Inputs may be any that keep to these rules, and one draw needn't show every extreme that they name: `lengths`: every sequence has 1024 or more live tokens; in every draw one sequence has all 4096. Offsets j - i <= 0 map into buckets below 16, offsets above 0 into the upper half.
All inputs are finite; a program needn't handle non-finite values.
Results may differ from a plain program's by a relative error of at most 0.02.
Values may be sent and summed in bfloat16 or wider, within the bound.
No kernel may reach another device: no remote copies, remote signals or barrier semaphores. Data moves between devices by JAX's collectives and lax.ppermute only.
A program may use at most 256 MiB of HBM per device.

v0:
```python
import jax
import jax.numpy as jnp
from jax import lax
from jax.sharding import PartitionSpec as P

EPSILON = 1e-06
MASKED = -1e30
HIGH = lax.Precision.HIGHEST


def shifted(block, axis, distance):
    devices = range(lax.axis_size(axis))
    route = [((i - distance) % len(devices), i) for i in devices]
    return lax.ppermute(block, axis, route)


def row_scale(values):
    return lax.rsqrt(jnp.mean(values * values, axis=-1, keepdims=True) + EPSILON)


def normalize(values, gain):
    return values * row_scale(values) * gain


def skew_expand(offset_bias, length):
    count = offset_bias.shape[0]
    padded = jnp.pad(offset_bias, ((0, 0), (0, 1)))
    tiled = jnp.tile(padded, (1, length))[:, : length * (2 * length - 1)]
    return tiled.reshape(count, length, 2 * length - 1)[:, :, length - 1 :]


def diagonal_sums(grid, length):
    count = grid.shape[0]
    wide = jnp.pad(grid, ((0, 0), (0, 0), (length - 1, 0))).reshape(
        count, length * (2 * length - 1)
    )
    wide = jnp.pad(wide, ((0, 0), (0, length)))
    return jnp.sum(wide.reshape(count, length, 2 * length), axis=1)[:, : 2 * length - 1]


def bucket_onehot(offset_start, length, buckets, bucket_count):
    reach = (buckets.shape[0] + 1) // 2
    offsets = offset_start + jnp.arange(2 * length - 1, dtype=jnp.int32) - (length - 1)
    spots = jnp.clip(offsets, 1 - reach, reach - 1) + (reach - 1)
    table_spots = jnp.arange(buckets.shape[0], dtype=jnp.int32)
    chosen = jnp.sum(jnp.where(spots[:, None] == table_spots[None, :], buckets[None, :], 0), axis=1)
    return chosen[:, None] == jnp.arange(bucket_count, dtype=jnp.int32)[None, :]


def block_scores(query3, keys3, table, onehot, key_live, length):
    scores = jnp.einsum("ihd,jhd->hij", query3, keys3, preferred_element_type=jnp.float32)
    offset_bias = jnp.einsum(
        "ob,bh->ho", onehot.astype(jnp.bfloat16), table, preferred_element_type=jnp.float32
    )
    scores = scores + skew_expand(offset_bias, length)
    return jnp.where(key_live[None, None, :], scores, MASKED)


def body(
    tokens,
    lengths,
    buckets,
    attention_gain,
    query_weight,
    key_weight,
    value_weight,
    output_weight,
    bias_table,
    feed_gain,
    gate_weight,
    up_weight,
    down_weight,
    cotangent,
):
    (
        gain_first,
        query_full,
        key_full,
        value_full,
        output_full,
        table_full,
        gain_second,
        gate_full,
        up_full,
        down_full,
    ) = (
        lax.all_gather(attention_gain, "wsh", axis=0, tiled=True),
        lax.all_gather(query_weight, "wsh", axis=0, tiled=True),
        lax.all_gather(key_weight, "wsh", axis=0, tiled=True),
        lax.all_gather(value_weight, "wsh", axis=0, tiled=True),
        lax.all_gather(output_weight, "wsh", axis=1, tiled=True),
        lax.all_gather(bias_table, "wsh", axis=0, tiled=True),
        lax.all_gather(feed_gain, "wsh", axis=0, tiled=True),
        lax.all_gather(gate_weight, "wsh", axis=1, tiled=True),
        lax.all_gather(up_weight, "wsh", axis=1, tiled=True),
        lax.all_gather(down_weight, "wsh", axis=0, tiled=True),
    )
    length = tokens.shape[1]
    heads = table_full.shape[1]
    bucket_count = table_full.shape[0]
    inner = query_full.shape[1]
    head_size = inner // heads
    seq_count = lengths.shape[1]
    wide_count = lax.axis_size("ctx")
    span = wide_count // seq_count
    here = lax.axis_index("ctx")
    my_seq = here % seq_count
    my_block = here // seq_count
    seq_pick = jnp.arange(seq_count, dtype=jnp.int32) == my_seq
    my_length = jnp.sum(jnp.where(seq_pick, lengths[0], 0))
    positions = jnp.arange(length, dtype=jnp.int32)
    live = (my_block * length + positions < my_length).astype(jnp.float32)[:, None]
    inputs = tokens[0].astype(jnp.float32)
    gain_one = gain_first.astype(jnp.float32)
    first = normalize(inputs, gain_one).astype(jnp.bfloat16)
    query = jnp.dot(first, query_full, preferred_element_type=jnp.float32).astype(jnp.bfloat16)
    keys = jnp.dot(first, key_full, preferred_element_type=jnp.float32).astype(jnp.bfloat16)
    values = jnp.dot(first, value_full, preferred_element_type=jnp.float32).astype(jnp.bfloat16)
    query3 = query.reshape(length, heads, head_size)

    def forward_step(carry, block_keys, block_values, key_block):
        run_max, run_total, running = carry
        onehot = bucket_onehot((key_block - my_block) * length, length, buckets, bucket_count)
        key_live = key_block * length + positions < my_length
        scores = block_scores(
            query3,
            block_keys.reshape(length, heads, head_size),
            table_full,
            onehot,
            key_live,
            length,
        )
        new_max = jnp.maximum(run_max, jnp.max(scores, axis=2))
        weights = jnp.exp(scores - new_max[:, :, None])
        factor = jnp.exp(run_max - new_max)
        run_total = run_total * factor + jnp.sum(weights, axis=2)
        update = jnp.einsum(
            "hij,jhd->ihd",
            weights.astype(jnp.bfloat16),
            block_values.reshape(length, heads, head_size),
            preferred_element_type=jnp.float32,
        )
        running = running * jnp.transpose(factor)[:, :, None] + update
        return (new_max, run_total, running)

    start_carry = (
        jnp.full((heads, length), MASKED, jnp.float32),
        jnp.zeros((heads, length), jnp.float32),
        jnp.zeros((length, heads, head_size), jnp.float32),
    )
    start_carry = forward_step(start_carry, keys, values, my_block)
    stored = ()

    def cycle_turn(turn, state):
        carry, block_keys, block_values, stored_blocks = state
        block_keys, block_values = shifted((block_keys, block_values), "ctx", seq_count)
        carry = forward_step(carry, block_keys, block_values, (my_block - turn) % span)
        return (carry, block_keys, block_values, stored_blocks)

    (run_max, run_total, running), _, _, stored = lax.fori_loop(
        1, span, cycle_turn, (start_carry, keys, values, stored)
    )
    log_total = run_max + jnp.log(run_total)
    attention = (running / jnp.transpose(run_total)[:, :, None]).reshape(length, inner)
    attention_low = attention.astype(jnp.bfloat16)
    branch = jnp.dot(attention_low, output_full, preferred_element_type=jnp.float32)
    middle = inputs + live * branch
    gain_two = gain_second.astype(jnp.float32)
    second = normalize(middle, gain_two).astype(jnp.bfloat16)
    gate = jnp.dot(second, gate_full, preferred_element_type=jnp.float32)
    up = jnp.dot(second, up_full, preferred_element_type=jnp.float32)
    hidden = (jax.nn.gelu(gate, approximate=True) * up).astype(jnp.bfloat16)
    feed = jnp.dot(hidden, down_full, preferred_element_type=jnp.float32)
    result = (middle + live * feed).astype(jnp.bfloat16)
    outer = live * cotangent[0].astype(jnp.float32)
    outer_low = outer.astype(jnp.bfloat16)
    down_grad = jnp.einsum("tf,td->fd", hidden, outer_low, preferred_element_type=jnp.float32)
    hidden_grad = jnp.einsum("td,fd->tf", outer_low, down_full, preferred_element_type=jnp.float32)

    def gated(gate_in, up_in):
        return jax.nn.gelu(gate_in, approximate=True) * up_in

    _, gate_pull = jax.vjp(gated, gate, up)
    gate_back, up_back = gate_pull(hidden_grad)
    gate_low = gate_back.astype(jnp.bfloat16)
    up_low = up_back.astype(jnp.bfloat16)
    gate_grad = jnp.einsum("td,tf->df", second, gate_low, preferred_element_type=jnp.float32)
    up_grad = jnp.einsum("td,tf->df", second, up_low, preferred_element_type=jnp.float32)
    second_grad = jnp.einsum(
        "tf,df->td", gate_low, gate_full, preferred_element_type=jnp.float32
    ) + jnp.einsum("tf,df->td", up_low, up_full, preferred_element_type=jnp.float32)
    _, norm_pull = jax.vjp(normalize, middle, gain_two)
    middle_back, gain_two_grad = norm_pull(second_grad)
    middle_grad = outer + middle_back
    branch_low = (live * middle_grad).astype(jnp.bfloat16)
    output_grad = jnp.einsum(
        "ti,td->id", attention_low, branch_low, preferred_element_type=jnp.float32
    )
    attention_grad = jnp.einsum(
        "td,id->ti", branch_low, output_full, preferred_element_type=jnp.float32
    ).astype(jnp.bfloat16)
    attention_grad3 = attention_grad.reshape(length, heads, head_size)
    delta = jnp.transpose(
        jnp.sum(
            (attention_grad.astype(jnp.float32) * attention).reshape(length, heads, head_size),
            axis=2,
        )
    )

    def backward_step(block_keys, block_values, key_block):
        keys3 = block_keys.reshape(length, heads, head_size)
        values3 = block_values.reshape(length, heads, head_size)
        onehot = bucket_onehot((key_block - my_block) * length, length, buckets, bucket_count)
        key_live = key_block * length + positions < my_length
        scores = block_scores(query3, keys3, table_full, onehot, key_live, length)
        probs = jnp.exp(scores - log_total[:, :, None])
        prob_grad = jnp.einsum(
            "ihd,jhd->hij", attention_grad3, values3, preferred_element_type=jnp.float32
        )
        score_grad = (probs * (prob_grad - delta[:, :, None])).astype(jnp.bfloat16)
        part_query = jnp.einsum(
            "hij,jhd->ihd", score_grad, keys3, preferred_element_type=jnp.float32
        )
        part_keys = jnp.einsum(
            "hij,ihd->jhd", score_grad, query3, preferred_element_type=jnp.float32
        )
        part_values = jnp.einsum(
            "hij,ihd->jhd",
            probs.astype(jnp.bfloat16),
            attention_grad3,
            preferred_element_type=jnp.float32,
        )
        part_table = jnp.einsum(
            "ho,ob->bh",
            diagonal_sums(score_grad.astype(jnp.float32), length),
            onehot.astype(jnp.float32),
            precision=HIGH,
        )
        return (
            part_query.reshape(length, inner),
            part_keys.reshape(length, inner),
            part_values.reshape(length, inner),
            part_table,
        )

    def back_turn(turn, state):
        block_keys, block_values, keys_sum, values_sum, query_sum, table_sum = state
        part_query, part_keys, part_values, part_table = backward_step(
            block_keys, block_values, (my_block - turn) % span
        )
        keys_next = keys_sum + part_keys
        values_next = values_sum + part_values
        keys_sum, values_sum = (
            shifted(keys_next.astype(jnp.bfloat16), "ctx", seq_count).astype(keys_next.dtype),
            shifted(values_next.astype(jnp.bfloat16), "ctx", seq_count).astype(values_next.dtype),
        )
        block_keys, block_values = shifted((block_keys, block_values), "ctx", seq_count)
        return (
            block_keys,
            block_values,
            keys_sum,
            values_sum,
            query_sum + part_query,
            table_sum + part_table,
        )

    zeros_rows = jnp.zeros((length, inner), jnp.float32)
    back_state = (
        keys,
        values,
        zeros_rows,
        zeros_rows,
        zeros_rows,
        jnp.zeros((bucket_count, heads), jnp.float32),
    )
    _, _, keys_sum, values_sum, query_sum, table_grad = lax.fori_loop(
        0, span, back_turn, back_state
    )
    query_low = query_sum.astype(jnp.bfloat16)
    keys_low = keys_sum.astype(jnp.bfloat16)
    values_low = values_sum.astype(jnp.bfloat16)
    query_grad = jnp.einsum("td,ti->di", first, query_low, preferred_element_type=jnp.float32)
    key_grad = jnp.einsum("td,ti->di", first, keys_low, preferred_element_type=jnp.float32)
    value_grad = jnp.einsum("td,ti->di", first, values_low, preferred_element_type=jnp.float32)
    first_grad = (
        jnp.einsum("ti,di->td", query_low, query_full, preferred_element_type=jnp.float32)
        + jnp.einsum("ti,di->td", keys_low, key_full, preferred_element_type=jnp.float32)
        + jnp.einsum("ti,di->td", values_low, value_full, preferred_element_type=jnp.float32)
    )
    _, first_pull = jax.vjp(normalize, inputs, gain_one)
    inputs_back, gain_one_grad = first_pull(first_grad)
    input_gradient = (middle_grad + inputs_back).astype(jnp.bfloat16)
    small = lax.psum((gain_one_grad, table_grad, gain_two_grad), "ctx")
    wide = (
        lax.psum_scatter(query_grad, "ctx", scatter_dimension=1, tiled=True),
        lax.psum_scatter(key_grad, "ctx", scatter_dimension=1, tiled=True),
        lax.psum_scatter(value_grad, "ctx", scatter_dimension=1, tiled=True),
        lax.psum_scatter(output_grad, "ctx", scatter_dimension=0, tiled=True),
        lax.psum_scatter(gate_grad, "ctx", scatter_dimension=1, tiled=True),
        lax.psum_scatter(up_grad, "ctx", scatter_dimension=1, tiled=True),
        lax.psum_scatter(down_grad, "ctx", scatter_dimension=0, tiled=True),
    )
    final = (
        lax.psum_scatter(
            small[0].astype(jnp.bfloat16), "wsh", scatter_dimension=0, tiled=True
        ).astype(jnp.float32),
        lax.psum_scatter(
            small[1].astype(jnp.bfloat16), "wsh", scatter_dimension=0, tiled=True
        ).astype(jnp.float32),
        lax.psum_scatter(
            small[2].astype(jnp.bfloat16), "wsh", scatter_dimension=0, tiled=True
        ).astype(jnp.float32),
        lax.psum_scatter(
            wide[0].astype(jnp.bfloat16), "wsh", scatter_dimension=0, tiled=True
        ).astype(jnp.float32),
        lax.psum_scatter(
            wide[1].astype(jnp.bfloat16), "wsh", scatter_dimension=0, tiled=True
        ).astype(jnp.float32),
        lax.psum_scatter(
            wide[2].astype(jnp.bfloat16), "wsh", scatter_dimension=0, tiled=True
        ).astype(jnp.float32),
        lax.psum_scatter(
            wide[3].astype(jnp.bfloat16), "wsh", scatter_dimension=1, tiled=True
        ).astype(jnp.float32),
        lax.psum_scatter(
            wide[4].astype(jnp.bfloat16), "wsh", scatter_dimension=1, tiled=True
        ).astype(jnp.float32),
        lax.psum_scatter(
            wide[5].astype(jnp.bfloat16), "wsh", scatter_dimension=1, tiled=True
        ).astype(jnp.float32),
        lax.psum_scatter(
            wide[6].astype(jnp.bfloat16), "wsh", scatter_dimension=0, tiled=True
        ).astype(jnp.float32),
    )
    gain_one_out, table_out, gain_two_out = (final[0], final[1], final[2])
    query_out, key_out, value_out, output_out = (final[3], final[4], final[5], final[6])
    gate_out, up_out, down_out = (final[7], final[8], final[9])
    return (
        result[None],
        input_gradient[None],
        gain_one_out,
        query_out,
        key_out,
        value_out,
        output_out,
        table_out,
        gain_two_out,
        gate_out,
        up_out,
        down_out,
    )


def solution(mesh):
    placed = (
        P("wsh", "ctx", None),
        P("wsh", None),
        P(),
        P("wsh"),
        P("wsh", None),
        P("wsh", None),
        P("wsh", None),
        P(None, "wsh"),
        P("wsh", None),
        P("wsh"),
        P(None, "wsh"),
        P(None, "wsh"),
        P("wsh", None),
        P("wsh", "ctx", None),
    )
    return jax.shard_map(
        body,
        mesh=mesh,
        in_specs=placed,
        out_specs=(
            P("wsh", "ctx", None),
            P("wsh", "ctx", None),
            P("wsh"),
            P("wsh", "ctx"),
            P("wsh", "ctx"),
            P("wsh", "ctx"),
            P("ctx", "wsh"),
            P("wsh", None),
            P("wsh"),
            P(None, ("ctx", "wsh")),
            P(None, ("ctx", "wsh")),
            P(("ctx", "wsh"), None),
        ),
        check_vma=False,
    )
```

profile of v0, /device:TPU:0, one launch (start us, length us, event | category | flops | bytes accessed | tf_op | source)
XLA Modules:
  0.0 2166.0 jit_solution(2266062317483967884)
XLA Ops:
  12.0 5.2 all-gather
  22.4 4.8 reshape.279
  33.7 5.2 all-reduce.11
  43.6 14.7 all-gather.11.cloned.1.call-done
  65.3 16.8 all-gather.13.cloned.1.call-done
  89.0 317.9 %while.50 = (s32[]{:T(128)}, f32[6,256]{1,0:T(8,128)S(1)}, f32[6,256]{1,0:T(8,128)S(1)}, f32[256,6,64]{0,2,1:T(8,128)}, bf16[256,384]{0,1:T(8,128)(2,1)}, /*inde...) while((s32[]{:T(128)}, f32[6,256]{1,0:T(8,128)S(1)}, ...), condition=%wide.region_8.9_spmd.clone, body=%wide.region_4.8_spmd.clone.sunk | while | flops 104222576 | bytes 41623364 | solution.py:160
  95.8 4.8 reshape.332
  117.2 5.7 reshape.332
  139.4 4.8 reshape.332
  160.4 4.8 reshape.332
  181.5 4.8 reshape.332
  202.5 4.8 reshape.332
  243.6 5.4 reshape.332
  265.4 4.8 reshape.332
  286.4 4.8 reshape.332
  328.5 4.8 reshape.332
  370.6 4.8 reshape.332
  392.2 4.8 reshape.332
  411.8 9.1 fusion.83
  421.0 9.1 fusion.84
  430.0 71.0 %all-gather.21.cloned.1.call-done = bf16[3584,1472]{0,1:T(8,128)(2,1)} async-done(((bf16[1792,1472]{0,1:T(8,128)(2,1)}), bf16[3584,1472]{0,1:T(8,128)(2,1)}) %all-gather.21.cloned.1.call-update) | async-done | bytes 10551312 | tf_op jit(solution)/shard_map/all_gather | solution.py:96
  501.1 12.1 multiply_convert_fusion.1
  513.2 7.0 fusion.85
  528.0 569.6 %while.51 = (s32[]{:T(128)}, bf16[256,384]{0,1:T(8,128)(2,1)}, bf16[256,384]{0,1:T(8,128)(2,1)}, f32[256,384]{0,1:T(8,128)}, f32[256,384]{0,1:T(8,128)}, /*index...) while((s32[]{:T(128)}, bf16[256,384]{0,1:T(8,128)(2,1)}, ...), condition=%wide.region_15.16_spmd.clone, body=%wide.region_12.15_spmd.clone.sunk | while | flops 258763216 | bytes 65157164 | solution.py:276
  752.7 4.8 reshape.334
  788.6 4.8 reshape.334
  1001.5 4.8 reshape.334
  1037.4 4.8 reshape.334
  1073.2 4.8 reshape.334
  1111.8 10.9 fusion.86
  1122.8 10.9 fusion.87
  1134.8 10.8 fusion.49
  1151.8 61.6 %all-reduce.9 = (bf16[1472]{0:T(1024)(128)(2,1)S(1)}, bf16[32,6]{0,1:T(8,128)(2,1)S(1)}, bf16[1472]{0:T(1024)(128)(2,1)S(1)}) all-reduce(f32[1472]{0:T(1024)S(1)} %get-tuple-element.870, f32[32,6]{0,1:T(8,128)S(1)} %copy-done.47, f32[1472]{0:T(1024)S(1)} %copy-done.44), channel_id=1, replica_groups=mesh['ctx'=16,'wsh'=2] {'ctx'}, use_global_device_ids=true, to_apply=%region_18.19 | all-reduce | flops 3136 | bytes 18816 | tf_op jit(solution)/shard_map/psum | solution.py:293
  1216.2 14.2 reduce-scatter.28.cloned.1.call-done
  1232.3 63.7 %reduce-scatter.30.cloned.1.call-done = f32[1472,24]{0,1:T(8,128)} async-done(((f32[1472,384]{0,1:T(8,128)}), f32[1472,24]{0,1:T(8,128)}) %reduce-scatter.30.cloned.1.call-update) | async-done | bytes 141328 | tf_op jit(solution)/shard_map/reduce_scatter | solution.py:297
  1297.9 64.4 %reduce-scatter.32.cloned.1.call-done = f32[24,1472]{1,0:T(8,128)} async-done(((f32[384,1472]{1,0:T(8,128)}), f32[24,1472]{1,0:T(8,128)}) %reduce-scatter.32.cloned.1.call-update) | async-done | bytes 141328 | tf_op jit(solution)/shard_map/reduce_scatter | solution.py:298
  1364.2 219.8 %reduce-scatter.34.cloned.1.call-done = f32[1472,224]{0,1:T(8,128)} async-done(((f32[1472,3584]{0,1:T(8,128)}), f32[1472,224]{0,1:T(8,128)}) %reduce-scatter.34.cloned.1.call-update) | async-done | bytes 1318928 | tf_op jit(solution)/shard_map/reduce_scatter | solution.py:299
  1586.3 219.6 %reduce-scatter.38.cloned.1.call-done = f32[1472,224]{0,1:T(8,128)} async-done(((f32[1472,3584]{0,1:T(8,128)}), f32[1472,224]{0,1:T(8,128)}) %reduce-scatter.38.cloned.1.call-update) | async-done | bytes 1318928 | tf_op jit(solution)/shard_map/reduce_scatter | solution.py:300
  1808.8 218.8 %reduce-scatter.42.cloned.1.call-done = f32[224,1472]{1,0:T(8,128)} async-done(((f32[3584,1472]{1,0:T(8,128)}), f32[224,1472]{1,0:T(8,128)}) %reduce-scatter.42.cloned.1.call-update) | async-done | bytes 1318928 | tf_op jit(solution)/shard_map/reduce_scatter | solution.py:301
  2032.6 5.2 all-reduce.10
  2038.5 8.7 fusion.32
  2048.6 6.1 reduce-scatter.46.cloned.1.call-done
  2056.4 13.4 reduce-scatter.48.cloned.1.call-done
  2071.4 13.4 reduce-scatter.50.cloned.1.call-done
  2086.5 13.5 reduce-scatter.52.cloned.1.call-done
  2101.7 17.4 reduce-scatter.36.cloned.1.call-done
  2121.0 17.3 reduce-scatter.40.cloned.1.call-done
  2140.2 16.8 reduce-scatter.44.cloned.1.call-done
  (1523 shorter events, 898.6 us)
Async XLA Ops:
  7.2 33.8 %all-gather.9.cloned.1.call-start = ((), (), s32[]{:S(2)}) async-start(), calls=%async_computation.15 | async-start | bytes 1695744 | tf_op jit(solution)/shard_map/all_gather | solution.py:88
  7.9 50.4 %all-gather.11.cloned.1.call-start = ((), (), s32[]{:S(2)}) async-start(), calls=%async_computation.16 | async-start | bytes 1695744 | tf_op jit(solution)/shard_map/all_gather | solution.py:89
  8.7 73.5 %all-gather.13.cloned.1.call-start = ((), (), s32[]{:S(2)}) async-start(), calls=%async_computation.17 | async-start | bytes 1695744 | tf_op jit(solution)/shard_map/all_gather | solution.py:90
  9.4 399.5 %all-gather.15.cloned.1.call-start = ((), (), s32[]{:S(2)}) async-start(), calls=%async_computation.18 | async-start | bytes 1695744 | tf_op jit(solution)/shard_map/all_gather | solution.py:91
  10.0 401.8 %all-gather.17.cloned.1.call-start = ((), (), s32[]{:S(2)}) async-start(), calls=%async_computation.19 | async-start | bytes 15826944 | tf_op jit(solution)/shard_map/all_gather | solution.py:94
  10.6 410.4 %all-gather.19.cloned.1.call-start = ((), (), s32[]{:S(2)}) async-start(), calls=%async_computation.20 | async-start | bytes 15826944 | tf_op jit(solution)/shard_map/all_gather | solution.py:95
  11.2 489.9 %all-gather.21.cloned.1.call-start = ((), (), s32[]{:S(2)}) async-start(), calls=%async_computation.21 | async-start | bytes 15826944 | tf_op jit(solution)/shard_map/all_gather | solution.py:96
  11.9 1202.3 %reduce-scatter.26.cloned.1.call-start = ((), (), s32[]{:S(2)}) async-start(), calls=%async_computation.22 | async-start | bytes 2506752 | tf_op jit(solution)/shard_map/reduce_scatter | solution.py:295
  529.1 34.9 %collective-permute-start.2 = (bf16[256,384]{0,1:T(8,128)(2,1)S(1)}, bf16[256,384]{0,1:T(8,128)(2,1)}, u32[]{:S(2)}, u32[]{:S(2)}) collective-permute-start(bf16[256,384]{0,1:T(8,128)(2,1)S(1)} %copy.139), channel_id=1, source_target_pairs={{30,0},{0,2},{2,4},{4,6},{6,8},{8,10},{10,12},{12,14},{14,16},{16,... | collective-permute-start | bytes 589832 | tf_op jit(solution)/shard_map/while/body/eval_jaxpr/ppermute | solution.py:14
  530.7 33.2 %collective-permute-start.3 = (bf16[256,384]{0,1:T(8,128)(2,1)}, bf16[256,384]{0,1:T(8,128)(2,1)}, u32[]{:S(2)}, u32[]{:S(2)}) collective-permute-start(bf16[256,384]{0,1:T(8,128)(2,1)} %copy.140), channel_id=1, source_target_pairs={{30,0},{0,2},{2,4},{4,6},{6,8},{8,10},{10,12},{12,14},{14,16},{16,... | collective-permute-start | bytes 589832 | tf_op jit(solution)/shard_map/while/body/eval_jaxpr/ppermute | solution.py:14
  564.9 34.9 %collective-permute-start.2 = (bf16[256,384]{0,1:T(8,128)(2,1)S(1)}, bf16[256,384]{0,1:T(8,128)(2,1)}, u32[]{:S(2)}, u32[]{:S(2)}) collective-permute-start(bf16[256,384]{0,1:T(8,128)(2,1)S(1)} %copy.139), channel_id=1, source_target_pairs={{30,0},{0,2},{2,4},{4,6},{6,8},{8,10},{10,12},{12,14},{14,16},{16,... | collective-permute-start | bytes 589832 | tf_op jit(solution)/shard_map/while/body/eval_jaxpr/ppermute | solution.py:14
  566.5 33.2 %collective-permute-start.3 = (bf16[256,384]{0,1:T(8,128)(2,1)}, bf16[256,384]{0,1:T(8,128)(2,1)}, u32[]{:S(2)}, u32[]{:S(2)}) collective-permute-start(bf16[256,384]{0,1:T(8,128)(2,1)} %copy.140), channel_id=1, source_target_pairs={{30,0},{0,2},{2,4},{4,6},{6,8},{8,10},{10,12},{12,14},{14,16},{16,... | collective-permute-start | bytes 589832 | tf_op jit(solution)/shard_map/while/body/eval_jaxpr/ppermute | solution.py:14
  600.7 34.9 %collective-permute-start.2 = (bf16[256,384]{0,1:T(8,128)(2,1)S(1)}, bf16[256,384]{0,1:T(8,128)(2,1)}, u32[]{:S(2)}, u32[]{:S(2)}) collective-permute-start(bf16[256,384]{0,1:T(8,128)(2,1)S(1)} %copy.139), channel_id=1, source_target_pairs={{30,0},{0,2},{2,4},{4,6},{6,8},{8,10},{10,12},{12,14},{14,16},{16,... | collective-permute-start | bytes 589832 | tf_op jit(solution)/shard_map/while/body/eval_jaxpr/ppermute | solution.py:14
  602.4 33.2 %collective-permute-start.3 = (bf16[256,384]{0,1:T(8,128)(2,1)}, bf16[256,384]{0,1:T(8,128)(2,1)}, u32[]{:S(2)}, u32[]{:S(2)}) collective-permute-start(bf16[256,384]{0,1:T(8,128)(2,1)} %copy.140), channel_id=1, source_target_pairs={{30,0},{0,2},{2,4},{4,6},{6,8},{8,10},{10,12},{12,14},{14,16},{16,... | collective-permute-start | bytes 589832 | tf_op jit(solution)/shard_map/while/body/eval_jaxpr/ppermute | solution.py:14
  636.5 33.9 %collective-permute-start.2 = (bf16[256,384]{0,1:T(8,128)(2,1)S(1)}, bf16[256,384]{0,1:T(8,128)(2,1)}, u32[]{:S(2)}, u32[]{:S(2)}) collective-permute-start(bf16[256,384]{0,1:T(8,128)(2,1)S(1)} %copy.139), channel_id=1, source_target_pairs={{30,0},{0,2},{2,4},{4,6},{6,8},{8,10},{10,12},{12,14},{14,16},{16,... | collective-permute-start | bytes 589832 | tf_op jit(solution)/shard_map/while/body/eval_jaxpr/ppermute | solution.py:14
  671.4 34.9 %collective-permute-start.2 = (bf16[256,384]{0,1:T(8,128)(2,1)S(1)}, bf16[256,384]{0,1:T(8,128)(2,1)}, u32[]{:S(2)}, u32[]{:S(2)}) collective-permute-start(bf16[256,384]{0,1:T(8,128)(2,1)S(1)} %copy.139), channel_id=1, source_target_pairs={{30,0},{0,2},{2,4},{4,6},{6,8},{8,10},{10,12},{12,14},{14,16},{16,... | collective-permute-start | bytes 589832 | tf_op jit(solution)/shard_map/while/body/eval_jaxpr/ppermute | solution.py:14
  673.0 33.2 %collective-permute-start.3 = (bf16[256,384]{0,1:T(8,128)(2,1)}, bf16[256,384]{0,1:T(8,128)(2,1)}, u32[]{:S(2)}, u32[]{:S(2)}) collective-permute-start(bf16[256,384]{0,1:T(8,128)(2,1)} %copy.140), channel_id=1, source_target_pairs={{30,0},{0,2},{2,4},{4,6},{6,8},{8,10},{10,12},{12,14},{14,16},{16,... | collective-permute-start | bytes 589832 | tf_op jit(solution)/shard_map/while/body/eval_jaxpr/ppermute | solution.py:14
  707.2 34.9 %collective-permute-start.2 = (bf16[256,384]{0,1:T(8,128)(2,1)S(1)}, bf16[256,384]{0,1:T(8,128)(2,1)}, u32[]{:S(2)}, u32[]{:S(2)}) collective-permute-start(bf16[256,384]{0,1:T(8,128)(2,1)S(1)} %copy.139), channel_id=1, source_target_pairs={{30,0},{0,2},{2,4},{4,6},{6,8},{8,10},{10,12},{12,14},{14,16},{16,... | collective-permute-start | bytes 589832 | tf_op jit(solution)/shard_map/while/body/eval_jaxpr/ppermute | solution.py:14
  708.9 33.2 %collective-permute-start.3 = (bf16[256,384]{0,1:T(8,128)(2,1)}, bf16[256,384]{0,1:T(8,128)(2,1)}, u32[]{:S(2)}, u32[]{:S(2)}) collective-permute-start(bf16[256,384]{0,1:T(8,128)(2,1)} %copy.140), channel_id=1, source_target_pairs={{30,0},{0,2},{2,4},{4,6},{6,8},{8,10},{10,12},{12,14},{14,16},{16,... | collective-permute-start | bytes 589832 | tf_op jit(solution)/shard_map/while/body/eval_jaxpr/ppermute | solution.py:14
  743.0 34.9 %collective-permute-start.2 = (bf16[256,384]{0,1:T(8,128)(2,1)S(1)}, bf16[256,384]{0,1:T(8,128)(2,1)}, u32[]{:S(2)}, u32[]{:S(2)}) collective-permute-start(bf16[256,384]{0,1:T(8,128)(2,1)S(1)} %copy.139), channel_id=1, source_target_pairs={{30,0},{0,2},{2,4},{4,6},{6,8},{8,10},{10,12},{12,14},{14,16},{16,... | collective-permute-start | bytes 589832 | tf_op jit(solution)/shard_map/while/body/eval_jaxpr/ppermute | solution.py:14
  744.7 33.2 %collective-permute-start.3 = (bf16[256,384]{0,1:T(8,128)(2,1)}, bf16[256,384]{0,1:T(8,128)(2,1)}, u32[]{:S(2)}, u32[]{:S(2)}) collective-permute-start(bf16[256,384]{0,1:T(8,128)(2,1)} %copy.140), channel_id=1, source_target_pairs={{30,0},{0,2},{2,4},{4,6},{6,8},{8,10},{10,12},{12,14},{14,16},{16,... | collective-permute-start | bytes 589832 | tf_op jit(solution)/shard_map/while/body/eval_jaxpr/ppermute | solution.py:14
  778.8 33.9 %collective-permute-start.2 = (bf16[256,384]{0,1:T(8,128)(2,1)S(1)}, bf16[256,384]{0,1:T(8,128)(2,1)}, u32[]{:S(2)}, u32[]{:S(2)}) collective-permute-start(bf16[256,384]{0,1:T(8,128)(2,1)S(1)} %copy.139), channel_id=1, source_target_pairs={{30,0},{0,2},{2,4},{4,6},{6,8},{8,10},{10,12},{12,14},{14,16},{16,... | collective-permute-start | bytes 589832 | tf_op jit(solution)/shard_map/while/body/eval_jaxpr/ppermute | solution.py:14
  813.7 34.9 %collective-permute-start.2 = (bf16[256,384]{0,1:T(8,128)(2,1)S(1)}, bf16[256,384]{0,1:T(8,128)(2,1)}, u32[]{:S(2)}, u32[]{:S(2)}) collective-permute-start(bf16[256,384]{0,1:T(8,128)(2,1)S(1)} %copy.139), channel_id=1, source_target_pairs={{30,0},{0,2},{2,4},{4,6},{6,8},{8,10},{10,12},{12,14},{14,16},{16,... | collective-permute-start | bytes 589832 | tf_op jit(solution)/shard_map/while/body/eval_jaxpr/ppermute | solution.py:14
  815.4 33.2 %collective-permute-start.3 = (bf16[256,384]{0,1:T(8,128)(2,1)}, bf16[256,384]{0,1:T(8,128)(2,1)}, u32[]{:S(2)}, u32[]{:S(2)}) collective-permute-start(bf16[256,384]{0,1:T(8,128)(2,1)} %copy.140), channel_id=1, source_target_pairs={{30,0},{0,2},{2,4},{4,6},{6,8},{8,10},{10,12},{12,14},{14,16},{16,... | collective-permute-start | bytes 589832 | tf_op jit(solution)/shard_map/while/body/eval_jaxpr/ppermute | solution.py:14
  849.5 34.9 %collective-permute-start.2 = (bf16[256,384]{0,1:T(8,128)(2,1)S(1)}, bf16[256,384]{0,1:T(8,128)(2,1)}, u32[]{:S(2)}, u32[]{:S(2)}) collective-permute-start(bf16[256,384]{0,1:T(8,128)(2,1)S(1)} %copy.139), channel_id=1, source_target_pairs={{30,0},{0,2},{2,4},{4,6},{6,8},{8,10},{10,12},{12,14},{14,16},{16,... | collective-permute-start | bytes 589832 | tf_op jit(solution)/shard_map/while/body/eval_jaxpr/ppermute | solution.py:14
  851.2 33.2 %collective-permute-start.3 = (bf16[256,384]{0,1:T(8,128)(2,1)}, bf16[256,384]{0,1:T(8,128)(2,1)}, u32[]{:S(2)}, u32[]{:S(2)}) collective-permute-start(bf16[256,384]{0,1:T(8,128)(2,1)} %copy.140), channel_id=1, source_target_pairs={{30,0},{0,2},{2,4},{4,6},{6,8},{8,10},{10,12},{12,14},{14,16},{16,... | collective-permute-start | bytes 589832 | tf_op jit(solution)/shard_map/while/body/eval_jaxpr/ppermute | solution.py:14
  885.3 34.9 %collective-permute-start.2 = (bf16[256,384]{0,1:T(8,128)(2,1)S(1)}, bf16[256,384]{0,1:T(8,128)(2,1)}, u32[]{:S(2)}, u32[]{:S(2)}) collective-permute-start(bf16[256,384]{0,1:T(8,128)(2,1)S(1)} %copy.139), channel_id=1, source_target_pairs={{30,0},{0,2},{2,4},{4,6},{6,8},{8,10},{10,12},{12,14},{14,16},{16,... | collective-permute-start | bytes 589832 | tf_op jit(solution)/shard_map/while/body/eval_jaxpr/ppermute | solution.py:14
  887.0 33.2 %collective-permute-start.3 = (bf16[256,384]{0,1:T(8,128)(2,1)}, bf16[256,384]{0,1:T(8,128)(2,1)}, u32[]{:S(2)}, u32[]{:S(2)}) collective-permute-start(bf16[256,384]{0,1:T(8,128)(2,1)} %copy.140), channel_id=1, source_target_pairs={{30,0},{0,2},{2,4},{4,6},{6,8},{8,10},{10,12},{12,14},{14,16},{16,... | collective-permute-start | bytes 589832 | tf_op jit(solution)/shard_map/while/body/eval_jaxpr/ppermute | solution.py:14
  921.2 33.9 %collective-permute-start.2 = (bf16[256,384]{0,1:T(8,128)(2,1)S(1)}, bf16[256,384]{0,1:T(8,128)(2,1)}, u32[]{:S(2)}, u32[]{:S(2)}) collective-permute-start(bf16[256,384]{0,1:T(8,128)(2,1)S(1)} %copy.139), channel_id=1, source_target_pairs={{30,0},{0,2},{2,4},{4,6},{6,8},{8,10},{10,12},{12,14},{14,16},{16,... | collective-permute-start | bytes 589832 | tf_op jit(solution)/shard_map/while/body/eval_jaxpr/ppermute | solution.py:14
  956.0 34.9 %collective-permute-start.2 = (bf16[256,384]{0,1:T(8,128)(2,1)S(1)}, bf16[256,384]{0,1:T(8,128)(2,1)}, u32[]{:S(2)}, u32[]{:S(2)}) collective-permute-start(bf16[256,384]{0,1:T(8,128)(2,1)S(1)} %copy.139), channel_id=1, source_target_pairs={{30,0},{0,2},{2,4},{4,6},{6,8},{8,10},{10,12},{12,14},{14,16},{16,... | collective-permute-start | bytes 589832 | tf_op jit(solution)/shard_map/while/body/eval_jaxpr/ppermute | solution.py:14
  991.8 34.9 %collective-permute-start.2 = (bf16[256,384]{0,1:T(8,128)(2,1)S(1)}, bf16[256,384]{0,1:T(8,128)(2,1)}, u32[]{:S(2)}, u32[]{:S(2)}) collective-permute-start(bf16[256,384]{0,1:T(8,128)(2,1)S(1)} %copy.139), channel_id=1, source_target_pairs={{30,0},{0,2},{2,4},{4,6},{6,8},{8,10},{10,12},{12,14},{14,16},{16,... | collective-permute-start | bytes 589832 | tf_op jit(solution)/shard_map/while/body/eval_jaxpr/ppermute | solution.py:14
  993.5 33.2 %collective-permute-start.3 = (bf16[256,384]{0,1:T(8,128)(2,1)}, bf16[256,384]{0,1:T(8,128)(2,1)}, u32[]{:S(2)}, u32[]{:S(2)}) collective-permute-start(bf16[256,384]{0,1:T(8,128)(2,1)} %copy.140), channel_id=1, source_target_pairs={{30,0},{0,2},{2,4},{4,6},{6,8},{8,10},{10,12},{12,14},{14,16},{16,... | collective-permute-start | bytes 589832 | tf_op jit(solution)/shard_map/while/body/eval_jaxpr/ppermute | solution.py:14
  1027.6 34.9 %collective-permute-start.2 = (bf16[256,384]{0,1:T(8,128)(2,1)S(1)}, bf16[256,384]{0,1:T(8,128)(2,1)}, u32[]{:S(2)}, u32[]{:S(2)}) collective-permute-start(bf16[256,384]{0,1:T(8,128)(2,1)S(1)} %copy.139), channel_id=1, source_target_pairs={{30,0},{0,2},{2,4},{4,6},{6,8},{8,10},{10,12},{12,14},{14,16},{16,... | collective-permute-start | bytes 589832 | tf_op jit(solution)/shard_map/while/body/eval_jaxpr/ppermute | solution.py:14
  1063.5 33.9 %collective-permute-start.2 = (bf16[256,384]{0,1:T(8,128)(2,1)S(1)}, bf16[256,384]{0,1:T(8,128)(2,1)}, u32[]{:S(2)}, u32[]{:S(2)}) collective-permute-start(bf16[256,384]{0,1:T(8,128)(2,1)S(1)} %copy.139), channel_id=1, source_target_pairs={{30,0},{0,2},{2,4},{4,6},{6,8},{8,10},{10,12},{12,14},{14,16},{16,... | collective-permute-start | bytes 589832 | tf_op jit(solution)/shard_map/while/body/eval_jaxpr/ppermute | solution.py:14
  1100.8 129.5 %reduce-scatter.28.cloned.1.call-start = ((), (), s32[]{:S(2)}) async-start(), calls=%async_computation.23 | async-start | bytes 2506752 | tf_op jit(solution)/shard_map/reduce_scatter | solution.py:296
  1104.2 191.7 %reduce-scatter.30.cloned.1.call-start = ((), (), s32[]{:S(2)}) async-start(), calls=%async_computation.24 | async-start | bytes 2506752 | tf_op jit(solution)/shard_map/reduce_scatter | solution.py:297
  1107.3 255.0 %reduce-scatter.32.cloned.1.call-start = ((), (), s32[]{:S(2)}) async-start(), calls=%async_computation.25 | async-start | bytes 2506752 | tf_op jit(solution)/shard_map/reduce_scatter | solution.py:298
  1110.7 473.2 %reduce-scatter.34.cloned.1.call-start = ((), (), s32[]{:S(2)}) async-start(), calls=%async_computation.26 | async-start | bytes 23396352 | tf_op jit(solution)/shard_map/reduce_scatter | solution.py:299
  1122.8 683.1 %reduce-scatter.38.cloned.1.call-start = ((), (), s32[]{:S(2)}) async-start(), calls=%async_computation.28 | async-start | bytes 23396352 | tf_op jit(solution)/shard_map/reduce_scatter | solution.py:300
  1133.7 893.9 %reduce-scatter.42.cloned.1.call-start = ((), (), s32[]{:S(2)}) async-start(), calls=%async_computation.30 | async-start | bytes 23396352 | tf_op jit(solution)/shard_map/reduce_scatter | solution.py:301
  1145.7 901.6 %reduce-scatter.54.cloned.1.call-start = ((), (), s32[]{:S(2)}) async-start(), calls=%async_computation.36 | async-start | bytes 12288
  1214.1 840.6 %reduce-scatter.46.cloned.1.call-start = ((), (), s32[]{:S(2)}) async-start(), calls=%async_computation.32 | async-start | bytes 565248
  1216.1 853.7 %reduce-scatter.48.cloned.1.call-start = ((), (), s32[]{:S(2)}) async-start(), calls=%async_computation.33 | async-start | bytes 565248
  1232.3 852.6 %reduce-scatter.50.cloned.1.call-start = ((), (), s32[]{:S(2)}) async-start(), calls=%async_computation.34 | async-start | bytes 565248
  1297.9 802.2 %reduce-scatter.52.cloned.1.call-start = ((), (), s32[]{:S(2)}) async-start(), calls=%async_computation.35 | async-start | bytes 565248
  1364.1 755.0 %reduce-scatter.36.cloned.1.call-start = ((), (), s32[]{:S(2)}) async-start(), calls=%async_computation.27 | async-start | bytes 1032192 | tf_op jit(solution)/shard_map/reduce_scatter | solution.py:325
  1586.2 552.1 %reduce-scatter.40.cloned.1.call-start = ((), (), s32[]{:S(2)}) async-start(), calls=%async_computation.29 | async-start | bytes 1032192 | tf_op jit(solution)/shard_map/reduce_scatter | solution.py:328
  1808.1 348.9 %reduce-scatter.44.cloned.1.call-start = ((), (), s32[]{:S(2)}) async-start(), calls=%async_computation.31 | async-start | bytes 1032192 | tf_op jit(solution)/shard_map/reduce_scatter | solution.py:331
  (317 other events, 2175.4 us)
Sparse Core Ops, SparseCore 0:
  9.6 24.9 all-gather.8
  36.0 22.2 all-gather.10
  59.9 22.2 all-gather.12
  83.5 22.2 all-gather.14
  107.2 130.3 all-gather.16
  239.0 130.2 all-gather.18
  370.8 130.2 all-gather.20
  1101.0 62.9 reduce-scatter.25
  1168.2 62.0 reduce-scatter.27
  1234.0 61.9 reduce-scatter.29
  1300.2 61.9 reduce-scatter.31
  1366.3 217.6 reduce-scatter.33
  1588.1 217.6 reduce-scatter.37
  1809.9 217.6 reduce-scatter.41
  2030.2 8.8 reduce-scatter.53
  2041.7 12.9 reduce-scatter.45
  2056.8 12.9 reduce-scatter.47
  2071.9 12.9 reduce-scatter.49
  2087.1 12.9 reduce-scatter.51
  2102.7 16.3 reduce-scatter.35
  2121.9 16.3 reduce-scatter.39
  2140.6 16.3 reduce-scatter.43
where the time goes:
time: 2180 us; the launch traced here: 2170 us
  waiting for transfers between devices  1010 us (46%)
  local copies, waits for them, and re-layouts  598 us (27%)
  matrix products  210 us (10%)
  other arithmetic  181 us (8%)
  blocking collectives  77.2 us (4%)
  starting transfers between devices  70.9 us (3%)
    while x578, local copies, waits for them, and re-layouts  255 us
    reduce_scatter x1, waiting for transfers between devices, body(): lax.psum_scatter(gate_grad, 'ctx', scatter_dimension=1, tiled=True)  220 us
    reduce_scatter x1, waiting for transfers between devices, body(): lax.psum_scatter(up_grad, 'ctx', scatter_dimension=1, tiled=True)  220 us
    reduce_scatter x1, waiting for transfers between devices, body(): lax.psum_scatter(down_grad, 'ctx', scatter_dimension=0, tiled=True)  219 us
    reshape x32, local copies, waits for them, and re-layouts, skew_expand(): return tiled.reshape(count, length, 2 * length - 1)[:, :, length - 1:]  154 us
    slice x32, local copies, waits for them, and re-layouts, skew_expand(): tiled = jnp.tile(padded, (1, length))[:, :length * (2 * length - 1)]  75.3 us
    all_gather x1, waiting for transfers between devices, body(): lax.all_gather(down_weight, 'wsh', axis=0, tiled=True)  71 us
    ppermute x94, starting transfers between devices, shifted(): return lax.ppermute(block, axis, route)  70 us
  transfers between devices with their start and end apart: 116, of which 16 were waited for; matrix products, arithmetic and copies ran while one was open for 43% of the time, Pallas kernels for 0%

commit v1 on v0

--- a/solution.py
+++ b/solution.py
@@ -6,6 +6,18 @@
 EPSILON = 1e-06
 MASKED = -1e30
 HIGH = lax.Precision.HIGHEST
+
+
+def collect(x, axis, dim):
+    ways, here = (lax.axis_size(axis), lax.axis_index(axis))
+    grown, reach = (x, 1)
+    while reach < ways:
+        theirs = lax.ppermute(grown, axis, [(d, d ^ reach) for d in range(ways)])
+        mine_first = jnp.concatenate([grown, theirs], axis=dim)
+        theirs_first = jnp.concatenate([theirs, grown], axis=dim)
+        grown = jnp.where(here & reach == 0, mine_first, theirs_first)
+        reach = 2 * reach
+    return grown
 
 
 def shifted(block, axis, distance):
@@ -93,7 +105,7 @@
         lax.all_gather(feed_gain, "wsh", axis=0, tiled=True),
         lax.all_gather(gate_weight, "wsh", axis=1, tiled=True),
         lax.all_gather(up_weight, "wsh", axis=1, tiled=True),
-        lax.all_gather(down_weight, "wsh", axis=0, tiled=True),
+        collect(down_weight, "wsh", 0),
     )
     length = tokens.shape[1]
     heads = table_full.shape[1]

time: 2180 us -> 2240 us (1.028)
  blocking collectives: 77.2 us -> 238 us
  waiting for transfers between devices: 1010 us -> 901 us
    all_gather x1, blocking collectives: 5.23 us -> 167 us  [body(): lax.all_gather(bias_table, 'wsh', axis=0, tiled=True)]
    all_gather x1 -> x0, waiting for transfers between devices: 71 us -> none  [body(): lax.all_gather(down_weight, 'wsh', axis=0, tiled=True)]
    unnamed x27 -> x26, waiting for transfers between devices: 51 us -> 56.1 us
  transfers between devices with their start and end apart: 116 -> 116, of which waited for: 16 -> 13; matrix products, arithmetic and copies ran while one was open for 43% -> 41% of each run, Pallas kernels for 0% -> 0%
where the time goes in v1:
time: 2240 us; the launch traced here: 2230 us
  waiting for transfers between devices  901 us (40%)
  local copies, waits for them, and re-layouts  593 us (26%)
  blocking collectives  238 us (11%)
  matrix products  216 us (10%)
  other arithmetic  181 us (8%)
  starting transfers between devices  74.6 us (3%)
    while x578, local copies, waits for them, and re-layouts  253 us
    reduce_scatter x1, waiting for transfers between devices, body(): lax.psum_scatter(gate_grad, 'ctx', scatter_dimension=1, tiled=True)  220 us
    reduce_scatter x1, waiting for transfers between devices, body(): lax.psum_scatter(up_grad, 'ctx', scatter_dimension=1, tiled=True)  219 us
    reduce_scatter x1, waiting for transfers between devices, body(): lax.psum_scatter(down_grad, 'ctx', scatter_dimension=0, tiled=True)  210 us
    all_gather x1, blocking collectives, body(): lax.all_gather(bias_table, 'wsh', axis=0, tiled=True)  167 us
    reshape x32, local copies, waits for them, and re-layouts, skew_expand(): return tiled.reshape(count, length, 2 * length - 1)[:, :, length - 1:]  153 us
    slice x32, local copies, waits for them, and re-layouts, skew_expand(): tiled = jnp.tile(padded, (1, length))[:, :length * (2 * length - 1)]  72.6 us
    ppermute x94, starting transfers between devices, shifted(): return lax.ppermute(block, axis, route)  70.8 us
  transfers between devices with their start and end apart: 116, of which 13 were waited for; matrix products, arithmetic and copies ran while one was open for 41% of the time, Pallas kernels for 0%

profile of v1, /device:TPU:0, one launch (start us, length us, event | category | flops | bytes accessed | tf_op | source)
XLA Modules:
  0.0 2227.7 jit_solution(6146108082645566348)
XLA Ops:
  13.8 167.4 %all-gather = bf16[2,16,6]{1,2,0:T(8,128)(2,1)S(1)} all-gather(bf16[1,16,6]{1,2,0:T(8,128)(2,1)S(1)} %bitcast.217), channel_id=1, replica_groups=mesh['ctx'=16,'wsh'=2] {'wsh'}, dimensions={0}, use_global_device_ids=true | all-gather | bytes 576 | tf_op jit(solution)/shard_map/all_gather | solution.py:104
  186.2 4.8 reshape.279
  197.5 5.5 all-reduce.11
  221.5 313.7 %while.50 = (s32[]{:T(128)}, f32[6,256]{1,0:T(8,128)S(1)}, f32[6,256]{1,0:T(8,128)S(1)}, f32[256,6,64]{0,2,1:T(8,128)}, bf16[256,384]{0,1:T(8,128)(2,1)}, /*inde...) while((s32[]{:T(128)}, f32[6,256]{1,0:T(8,128)S(1)}, ...), condition=%wide.region_8.9_spmd.clone, body=%wide.region_4.8_spmd.clone.sunk | while | flops 104222576 | bytes 41623364 | solution.py:172
  228.0 4.8 reshape.332
  249.0 4.8 reshape.332
  269.9 4.8 reshape.332
  290.9 4.8 reshape.332
  312.2 5.2 reshape.332
  333.6 4.8 reshape.332
  354.7 4.8 reshape.332
  374.1 4.8 reshape.332
  394.6 4.8 reshape.332
  415.6 4.8 reshape.332
  436.6 4.8 reshape.332
  457.8 4.8 reshape.332
  478.6 4.8 reshape.332
  499.7 4.8 reshape.332
  520.7 4.8 reshape.332
  540.2 9.1 fusion.85
  549.3 8.9 fusion.86
  558.2 17.2 multiply_convert_fusion.1
  575.4 6.4 fusion.87
  591.1 567.8 %while.51 = (s32[]{:T(128)}, bf16[256,384]{0,1:T(8,128)(2,1)}, bf16[256,384]{0,1:T(8,128)(2,1)}, f32[256,384]{0,1:T(8,128)}, f32[256,384]{0,1:T(8,128)}, /*index...) while((s32[]{:T(128)}, bf16[256,384]{0,1:T(8,128)(2,1)}, ...), condition=%wide.region_15.16_spmd.clone, body=%wide.region_12.15_spmd.clone.sunk | while | flops 258763216 | bytes 65157164 | solution.py:288
  600.4 4.8 reshape.334
  635.9 4.8 reshape.334
  672.1 4.8 reshape.334
  707.9 4.8 reshape.334
  1026.0 4.8 reshape.334
  1173.0 11.2 fusion.88
  1184.2 11.0 fusion.89
  1196.3 10.8 fusion.50
  1213.3 60.6 %all-reduce.9 = (bf16[1472]{0:T(1024)(128)(2,1)S(1)}, bf16[32,6]{0,1:T(8,128)(2,1)S(1)}, bf16[1472]{0:T(1024)(128)(2,1)S(1)}) all-reduce(f32[1472]{0:T(1024)S(1)} %get-tuple-element.870, f32[32,6]{0,1:T(8,128)S(1)} %copy-done.48, f32[1472]{0:T(1024)S(1)} %copy-done.45), channel_id=1, replica_groups=mesh['ctx'=16,'wsh'=2] {'ctx'}, use_global_device_ids=true, to_apply=%region_18.19 | all-reduce | flops 3136 | bytes 18816 | tf_op jit(solution)/shard_map/psum | solution.py:305
  1276.6 15.4 reduce-scatter.28.cloned.1.call-done
  1294.0 63.9 %reduce-scatter.30.cloned.1.call-done = f32[1472,24]{0,1:T(8,128)} async-done(((f32[1472,384]{0,1:T(8,128)}), f32[1472,24]{0,1:T(8,128)}) %reduce-scatter.30.cloned.1.call-update) | async-done | bytes 141328 | tf_op jit(solution)/shard_map/reduce_scatter | solution.py:309
  1359.8 64.2 %reduce-scatter.32.cloned.1.call-done = f32[24,1472]{1,0:T(8,128)} async-done(((f32[384,1472]{1,0:T(8,128)}), f32[24,1472]{1,0:T(8,128)}) %reduce-scatter.32.cloned.1.call-update) | async-done | bytes 141328 | tf_op jit(solution)/shard_map/reduce_scatter | solution.py:310
  1426.0 219.9 %reduce-scatter.34.cloned.1.call-done = f32[1472,224]{0,1:T(8,128)} async-done(((f32[1472,3584]{0,1:T(8,128)}), f32[1472,224]{0,1:T(8,128)}) %reduce-scatter.34.cloned.1.call-update) | async-done | bytes 1318928 | tf_op jit(solution)/shard_map/reduce_scatter | solution.py:311
  1648.2 219.4 %reduce-scatter.38.cloned.1.call-done = f32[1472,224]{0,1:T(8,128)} async-done(((f32[1472,3584]{0,1:T(8,128)}), f32[1472,224]{0,1:T(8,128)}) %reduce-scatter.38.cloned.1.call-update) | async-done | bytes 1318928 | tf_op jit(solution)/shard_map/reduce_scatter | solution.py:312
  1870.5 5.0 all-reduce.10
  1879.0 210.5 %reduce-scatter.42.cloned.1.call-done = f32[224,1472]{1,0:T(8,128)} async-done(((f32[3584,1472]{1,0:T(8,128)}), f32[224,1472]{1,0:T(8,128)}) %reduce-scatter.42.cloned.1.call-update) | async-done | bytes 1318928 | tf_op jit(solution)/shard_map/reduce_scatter | solution.py:313
  2091.8 10.9 fusion.32
  2104.1 12.5 reduce-scatter.46.cloned.1.call-done
  2118.3 13.4 reduce-scatter.48.cloned.1.call-done
  2133.3 13.4 reduce-scatter.50.cloned.1.call-done
  2148.4 13.4 reduce-scatter.52.cloned.1.call-done
  2163.5 17.6 reduce-scatter.36.cloned.1.call-done
  2182.9 17.2 reduce-scatter.40.cloned.1.call-done
  2202.0 16.8 reduce-scatter.44.cloned.1.call-done
  (1517 shorter events, 882.6 us)
Async XLA Ops:
  7.2 197.9 %all-gather.8.cloned.1.call-start = ((), (), s32[]{:S(2)}) async-start(), calls=%async_computation.15 | async-start | bytes 1695744 | tf_op jit(solution)/shard_map/all_gather | solution.py:100
  7.9 199.7 %all-gather.10.cloned.1.call-start = ((), (), s32[]{:S(2)}) async-start(), calls=%async_computation.16 | async-start | bytes 1695744 | tf_op jit(solution)/shard_map/all_gather | solution.py:101
  8.7 206.0 %all-gather.12.cloned.1.call-start = ((), (), s32[]{:S(2)}) async-start(), calls=%async_computation.17 | async-start | bytes 1695744 | tf_op jit(solution)/shard_map/all_gather | solution.py:102
  9.4 527.9 %all-gather.14.cloned.1.call-start = ((), (), s32[]{:S(2)}) async-start(), calls=%async_computation.18 | async-start | bytes 1695744 | tf_op jit(solution)/shard_map/all_gather | solution.py:103
  10.0 530.2 %all-gather.16.cloned.1.call-start = ((), (), s32[]{:S(2)}) async-start(), calls=%async_computation.19 | async-start | bytes 15826944 | tf_op jit(solution)/shard_map/all_gather | solution.py:106
  10.6 538.7 %all-gather.18.cloned.1.call-start = ((), (), s32[]{:S(2)}) async-start(), calls=%async_computation.20 | async-start | bytes 15826944 | tf_op jit(solution)/shard_map/all_gather | solution.py:107
  10.6 547.6 %collective-permute-start.6 = (bf16[1792,1472]{0,1:T(8,128)(2,1)}, bf16[1792,1472]{0,1:T(8,128)(2,1)}, u32[]{:S(2)}, u32[]{:S(2)}) collective-permute-start(bf16[1792,1472]{0,1:T(8,128)(2,1)} %param.30), channel_id=1, source_target_pairs={{0,1},{1,0},{2,3},{3,2},{4,5},{5,4},{6,7},{7,6},{8,9},{9,8},{10,11... | collective-permute-start | bytes 15826952 | tf_op jit(solution)/shard_map/ppermute | solution.py:15
  13.7 1261.0 %reduce-scatter.26.cloned.1.call-start = ((), (), s32[]{:S(2)}) async-start(), calls=%async_computation.21 | async-start | bytes 2506752 | tf_op jit(solution)/shard_map/reduce_scatter | solution.py:307
  592.2 33.0 %collective-permute-start.2 = (bf16[256,384]{0,1:T(8,128)(2,1)S(1)}, bf16[256,384]{0,1:T(8,128)(2,1)}, u32[]{:S(2)}, u32[]{:S(2)}) collective-permute-start(bf16[256,384]{0,1:T(8,128)(2,1)S(1)} %copy.139), channel_id=1, source_target_pairs={{30,0},{0,2},{2,4},{4,6},{6,8},{8,10},{10,12},{12,14},{14,16},{16,... | collective-permute-start | bytes 589832 | tf_op jit(solution)/shard_map/while/body/eval_jaxpr/ppermute | solution.py:26
  626.2 34.9 %collective-permute-start.2 = (bf16[256,384]{0,1:T(8,128)(2,1)S(1)}, bf16[256,384]{0,1:T(8,128)(2,1)}, u32[]{:S(2)}, u32[]{:S(2)}) collective-permute-start(bf16[256,384]{0,1:T(8,128)(2,1)S(1)} %copy.139), channel_id=1, source_target_pairs={{30,0},{0,2},{2,4},{4,6},{6,8},{8,10},{10,12},{12,14},{14,16},{16,... | collective-permute-start | bytes 589832 | tf_op jit(solution)/shard_map/while/body/eval_jaxpr/ppermute | solution.py:26
  627.9 33.2 %collective-permute-start.3 = (bf16[256,384]{0,1:T(8,128)(2,1)}, bf16[256,384]{0,1:T(8,128)(2,1)}, u32[]{:S(2)}, u32[]{:S(2)}) collective-permute-start(bf16[256,384]{0,1:T(8,128)(2,1)} %copy.140), channel_id=1, source_target_pairs={{30,0},{0,2},{2,4},{4,6},{6,8},{8,10},{10,12},{12,14},{14,16},{16,... | collective-permute-start | bytes 589832 | tf_op jit(solution)/shard_map/while/body/eval_jaxpr/ppermute | solution.py:26
  662.1 35.0 %collective-permute-start.2 = (bf16[256,384]{0,1:T(8,128)(2,1)S(1)}, bf16[256,384]{0,1:T(8,128)(2,1)}, u32[]{:S(2)}, u32[]{:S(2)}) collective-permute-start(bf16[256,384]{0,1:T(8,128)(2,1)S(1)} %copy.139), channel_id=1, source_target_pairs={{30,0},{0,2},{2,4},{4,6},{6,8},{8,10},{10,12},{12,14},{14,16},{16,... | collective-permute-start | bytes 589832 | tf_op jit(solution)/shard_map/while/body/eval_jaxpr/ppermute | solution.py:26
  663.7 33.4 %collective-permute-start.3 = (bf16[256,384]{0,1:T(8,128)(2,1)}, bf16[256,384]{0,1:T(8,128)(2,1)}, u32[]{:S(2)}, u32[]{:S(2)}) collective-permute-start(bf16[256,384]{0,1:T(8,128)(2,1)} %copy.140), channel_id=1, source_target_pairs={{30,0},{0,2},{2,4},{4,6},{6,8},{8,10},{10,12},{12,14},{14,16},{16,... | collective-permute-start | bytes 589832 | tf_op jit(solution)/shard_map/while/body/eval_jaxpr/ppermute | solution.py:26
  698.1 35.1 %collective-permute-start.2 = (bf16[256,384]{0,1:T(8,128)(2,1)S(1)}, bf16[256,384]{0,1:T(8,128)(2,1)}, u32[]{:S(2)}, u32[]{:S(2)}) collective-permute-start(bf16[256,384]{0,1:T(8,128)(2,1)S(1)} %copy.139), channel_id=1, source_target_pairs={{30,0},{0,2},{2,4},{4,6},{6,8},{8,10},{10,12},{12,14},{14,16},{16,... | collective-permute-start | bytes 589832 | tf_op jit(solution)/shard_map/while/body/eval_jaxpr/ppermute | solution.py:26
  699.8 33.4 %collective-permute-start.3 = (bf16[256,384]{0,1:T(8,128)(2,1)}, bf16[256,384]{0,1:T(8,128)(2,1)}, u32[]{:S(2)}, u32[]{:S(2)}) collective-permute-start(bf16[256,384]{0,1:T(8,128)(2,1)} %copy.140), channel_id=1, source_target_pairs={{30,0},{0,2},{2,4},{4,6},{6,8},{8,10},{10,12},{12,14},{14,16},{16,... | collective-permute-start | bytes 589832 | tf_op jit(solution)/shard_map/while/body/eval_jaxpr/ppermute | solution.py:26
  734.1 33.0 %collective-permute-start.2 = (bf16[256,384]{0,1:T(8,128)(2,1)S(1)}, bf16[256,384]{0,1:T(8,128)(2,1)}, u32[]{:S(2)}, u32[]{:S(2)}) collective-permute-start(bf16[256,384]{0,1:T(8,128)(2,1)S(1)} %copy.139), channel_id=1, source_target_pairs={{30,0},{0,2},{2,4},{4,6},{6,8},{8,10},{10,12},{12,14},{14,16},{16,... | collective-permute-start | bytes 589832 | tf_op jit(solution)/shard_map/while/body/eval_jaxpr/ppermute | solution.py:26
  768.0 34.9 %collective-permute-start.2 = (bf16[256,384]{0,1:T(8,128)(2,1)S(1)}, bf16[256,384]{0,1:T(8,128)(2,1)}, u32[]{:S(2)}, u32[]{:S(2)}) collective-permute-start(bf16[256,384]{0,1:T(8,128)(2,1)S(1)} %copy.139), channel_id=1, source_target_pairs={{30,0},{0,2},{2,4},{4,6},{6,8},{8,10},{10,12},{12,14},{14,16},{16,... | collective-permute-start | bytes 589832 | tf_op jit(solution)/shard_map/while/body/eval_jaxpr/ppermute | solution.py:26
  769.7 33.2 %collective-permute-start.3 = (bf16[256,384]{0,1:T(8,128)(2,1)}, bf16[256,384]{0,1:T(8,128)(2,1)}, u32[]{:S(2)}, u32[]{:S(2)}) collective-permute-start(bf16[256,384]{0,1:T(8,128)(2,1)} %copy.140), channel_id=1, source_target_pairs={{30,0},{0,2},{2,4},{4,6},{6,8},{8,10},{10,12},{12,14},{14,16},{16,... | collective-permute-start | bytes 589832 | tf_op jit(solution)/shard_map/while/body/eval_jaxpr/ppermute | solution.py:26
  803.9 35.0 %collective-permute-start.2 = (bf16[256,384]{0,1:T(8,128)(2,1)S(1)}, bf16[256,384]{0,1:T(8,128)(2,1)}, u32[]{:S(2)}, u32[]{:S(2)}) collective-permute-start(bf16[256,384]{0,1:T(8,128)(2,1)S(1)} %copy.139), channel_id=1, source_target_pairs={{30,0},{0,2},{2,4},{4,6},{6,8},{8,10},{10,12},{12,14},{14,16},{16,... | collective-permute-start | bytes 589832 | tf_op jit(solution)/shard_map/while/body/eval_jaxpr/ppermute | solution.py:26
  805.6 33.4 %collective-permute-start.3 = (bf16[256,384]{0,1:T(8,128)(2,1)}, bf16[256,384]{0,1:T(8,128)(2,1)}, u32[]{:S(2)}, u32[]{:S(2)}) collective-permute-start(bf16[256,384]{0,1:T(8,128)(2,1)} %copy.140), channel_id=1, source_target_pairs={{30,0},{0,2},{2,4},{4,6},{6,8},{8,10},{10,12},{12,14},{14,16},{16,... | collective-permute-start | bytes 589832 | tf_op jit(solution)/shard_map/while/body/eval_jaxpr/ppermute | solution.py:26
  839.9 35.1 %collective-permute-start.2 = (bf16[256,384]{0,1:T(8,128)(2,1)S(1)}, bf16[256,384]{0,1:T(8,128)(2,1)}, u32[]{:S(2)}, u32[]{:S(2)}) collective-permute-start(bf16[256,384]{0,1:T(8,128)(2,1)S(1)} %copy.139), channel_id=1, source_target_pairs={{30,0},{0,2},{2,4},{4,6},{6,8},{8,10},{10,12},{12,14},{14,16},{16,... | collective-permute-start | bytes 589832 | tf_op jit(solution)/shard_map/while/body/eval_jaxpr/ppermute | solution.py:26
  841.6 33.4 %collective-permute-start.3 = (bf16[256,384]{0,1:T(8,128)(2,1)}, bf16[256,384]{0,1:T(8,128)(2,1)}, u32[]{:S(2)}, u32[]{:S(2)}) collective-permute-start(bf16[256,384]{0,1:T(8,128)(2,1)} %copy.140), channel_id=1, source_target_pairs={{30,0},{0,2},{2,4},{4,6},{6,8},{8,10},{10,12},{12,14},{14,16},{16,... | collective-permute-start | bytes 589832 | tf_op jit(solution)/shard_map/while/body/eval_jaxpr/ppermute | solution.py:26
  909.9 34.9 %collective-permute-start.2 = (bf16[256,384]{0,1:T(8,128)(2,1)S(1)}, bf16[256,384]{0,1:T(8,128)(2,1)}, u32[]{:S(2)}, u32[]{:S(2)}) collective-permute-start(bf16[256,384]{0,1:T(8,128)(2,1)S(1)} %copy.139), channel_id=1, source_target_pairs={{30,0},{0,2},{2,4},{4,6},{6,8},{8,10},{10,12},{12,14},{14,16},{16,... | collective-permute-start | bytes 589832 | tf_op jit(solution)/shard_map/while/body/eval_jaxpr/ppermute | solution.py:26
  911.6 33.2 %collective-permute-start.3 = (bf16[256,384]{0,1:T(8,128)(2,1)}, bf16[256,384]{0,1:T(8,128)(2,1)}, u32[]{:S(2)}, u32[]{:S(2)}) collective-permute-start(bf16[256,384]{0,1:T(8,128)(2,1)} %copy.140), channel_id=1, source_target_pairs={{30,0},{0,2},{2,4},{4,6},{6,8},{8,10},{10,12},{12,14},{14,16},{16,... | collective-permute-start | bytes 589832 | tf_op jit(solution)/shard_map/while/body/eval_jaxpr/ppermute | solution.py:26
  945.8 35.0 %collective-permute-start.2 = (bf16[256,384]{0,1:T(8,128)(2,1)S(1)}, bf16[256,384]{0,1:T(8,128)(2,1)}, u32[]{:S(2)}, u32[]{:S(2)}) collective-permute-start(bf16[256,384]{0,1:T(8,128)(2,1)S(1)} %copy.139), channel_id=1, source_target_pairs={{30,0},{0,2},{2,4},{4,6},{6,8},{8,10},{10,12},{12,14},{14,16},{16,... | collective-permute-start | bytes 589832 | tf_op jit(solution)/shard_map/while/body/eval_jaxpr/ppermute | solution.py:26
  947.5 33.4 %collective-permute-start.3 = (bf16[256,384]{0,1:T(8,128)(2,1)}, bf16[256,384]{0,1:T(8,128)(2,1)}, u32[]{:S(2)}, u32[]{:S(2)}) collective-permute-start(bf16[256,384]{0,1:T(8,128)(2,1)} %copy.140), channel_id=1, source_target_pairs={{30,0},{0,2},{2,4},{4,6},{6,8},{8,10},{10,12},{12,14},{14,16},{16,... | collective-permute-start | bytes 589832 | tf_op jit(solution)/shard_map/while/body/eval_jaxpr/ppermute | solution.py:26
  981.8 35.1 %collective-permute-start.2 = (bf16[256,384]{0,1:T(8,128)(2,1)S(1)}, bf16[256,384]{0,1:T(8,128)(2,1)}, u32[]{:S(2)}, u32[]{:S(2)}) collective-permute-start(bf16[256,384]{0,1:T(8,128)(2,1)S(1)} %copy.139), channel_id=1, source_target_pairs={{30,0},{0,2},{2,4},{4,6},{6,8},{8,10},{10,12},{12,14},{14,16},{16,... | collective-permute-start | bytes 589832 | tf_op jit(solution)/shard_map/while/body/eval_jaxpr/ppermute | solution.py:26
  983.5 33.4 %collective-permute-start.3 = (bf16[256,384]{0,1:T(8,128)(2,1)}, bf16[256,384]{0,1:T(8,128)(2,1)}, u32[]{:S(2)}, u32[]{:S(2)}) collective-permute-start(bf16[256,384]{0,1:T(8,128)(2,1)} %copy.140), channel_id=1, source_target_pairs={{30,0},{0,2},{2,4},{4,6},{6,8},{8,10},{10,12},{12,14},{14,16},{16,... | collective-permute-start | bytes 589832 | tf_op jit(solution)/shard_map/while/body/eval_jaxpr/ppermute | solution.py:26
  1051.7 34.9 %collective-permute-start.2 = (bf16[256,384]{0,1:T(8,128)(2,1)S(1)}, bf16[256,384]{0,1:T(8,128)(2,1)}, u32[]{:S(2)}, u32[]{:S(2)}) collective-permute-start(bf16[256,384]{0,1:T(8,128)(2,1)S(1)} %copy.139), channel_id=1, source_target_pairs={{30,0},{0,2},{2,4},{4,6},{6,8},{8,10},{10,12},{12,14},{14,16},{16,... | collective-permute-start | bytes 589832 | tf_op jit(solution)/shard_map/while/body/eval_jaxpr/ppermute | solution.py:26
  1053.4 33.2 %collective-permute-start.3 = (bf16[256,384]{0,1:T(8,128)(2,1)}, bf16[256,384]{0,1:T(8,128)(2,1)}, u32[]{:S(2)}, u32[]{:S(2)}) collective-permute-start(bf16[256,384]{0,1:T(8,128)(2,1)} %copy.140), channel_id=1, source_target_pairs={{30,0},{0,2},{2,4},{4,6},{6,8},{8,10},{10,12},{12,14},{14,16},{16,... | collective-permute-start | bytes 589832 | tf_op jit(solution)/shard_map/while/body/eval_jaxpr/ppermute | solution.py:26
  1087.6 35.0 %collective-permute-start.2 = (bf16[256,384]{0,1:T(8,128)(2,1)S(1)}, bf16[256,384]{0,1:T(8,128)(2,1)}, u32[]{:S(2)}, u32[]{:S(2)}) collective-permute-start(bf16[256,384]{0,1:T(8,128)(2,1)S(1)} %copy.139), channel_id=1, source_target_pairs={{30,0},{0,2},{2,4},{4,6},{6,8},{8,10},{10,12},{12,14},{14,16},{16,... | collective-permute-start | bytes 589832 | tf_op jit(solution)/shard_map/while/body/eval_jaxpr/ppermute | solution.py:26
  1089.3 33.4 %collective-permute-start.3 = (bf16[256,384]{0,1:T(8,128)(2,1)}, bf16[256,384]{0,1:T(8,128)(2,1)}, u32[]{:S(2)}, u32[]{:S(2)}) collective-permute-start(bf16[256,384]{0,1:T(8,128)(2,1)} %copy.140), channel_id=1, source_target_pairs={{30,0},{0,2},{2,4},{4,6},{6,8},{8,10},{10,12},{12,14},{14,16},{16,... | collective-permute-start | bytes 589832 | tf_op jit(solution)/shard_map/while/body/eval_jaxpr/ppermute | solution.py:26
  1123.6 35.1 %collective-permute-start.2 = (bf16[256,384]{0,1:T(8,128)(2,1)S(1)}, bf16[256,384]{0,1:T(8,128)(2,1)}, u32[]{:S(2)}, u32[]{:S(2)}) collective-permute-start(bf16[256,384]{0,1:T(8,128)(2,1)S(1)} %copy.139), channel_id=1, source_target_pairs={{30,0},{0,2},{2,4},{4,6},{6,8},{8,10},{10,12},{12,14},{14,16},{16,... | collective-permute-start | bytes 589832 | tf_op jit(solution)/shard_map/while/body/eval_jaxpr/ppermute | solution.py:26
  1125.3 33.4 %collective-permute-start.3 = (bf16[256,384]{0,1:T(8,128)(2,1)}, bf16[256,384]{0,1:T(8,128)(2,1)}, u32[]{:S(2)}, u32[]{:S(2)}) collective-permute-start(bf16[256,384]{0,1:T(8,128)(2,1)} %copy.140), channel_id=1, source_target_pairs={{30,0},{0,2},{2,4},{4,6},{6,8},{8,10},{10,12},{12,14},{14,16},{16,... | collective-permute-start | bytes 589832 | tf_op jit(solution)/shard_map/while/body/eval_jaxpr/ppermute | solution.py:26
  1162.2 129.8 %reduce-scatter.28.cloned.1.call-start = ((), (), s32[]{:S(2)}) async-start(), calls=%async_computation.22 | async-start | bytes 2506752 | tf_op jit(solution)/shard_map/reduce_scatter | solution.py:308
  1165.5 192.4 %reduce-scatter.30.cloned.1.call-start = ((), (), s32[]{:S(2)}) async-start(), calls=%async_computation.23 | async-start | bytes 2506752 | tf_op jit(solution)/shard_map/reduce_scatter | solution.py:309
  1168.5 255.5 %reduce-scatter.32.cloned.1.call-start = ((), (), s32[]{:S(2)}) async-start(), calls=%async_computation.24 | async-start | bytes 2506752 | tf_op jit(solution)/shard_map/reduce_scatter | solution.py:310
  1171.8 474.0 %reduce-scatter.34.cloned.1.call-start = ((), (), s32[]{:S(2)}) async-start(), calls=%async_computation.25 | async-start | bytes 23396352 | tf_op jit(solution)/shard_map/reduce_scatter | solution.py:311
  1184.1 683.4 %reduce-scatter.38.cloned.1.call-start = ((), (), s32[]{:S(2)}) async-start(), calls=%async_computation.27 | async-start | bytes 23396352 | tf_op jit(solution)/shard_map/reduce_scatter | solution.py:312
  1195.2 894.3 %reduce-scatter.42.cloned.1.call-start = ((), (), s32[]{:S(2)}) async-start(), calls=%async_computation.29 | async-start | bytes 23396352 | tf_op jit(solution)/shard_map/reduce_scatter | solution.py:313
  1207.2 895.5 %reduce-scatter.54.cloned.1.call-start = ((), (), s32[]{:S(2)}) async-start(), calls=%async_computation.35 | async-start | bytes 12288
  1274.6 842.0 %reduce-scatter.46.cloned.1.call-start = ((), (), s32[]{:S(2)}) async-start(), calls=%async_computation.31 | async-start | bytes 565248
  1276.6 855.1 %reduce-scatter.48.cloned.1.call-start = ((), (), s32[]{:S(2)}) async-start(), calls=%async_computation.32 | async-start | bytes 565248
  1293.9 852.8 %reduce-scatter.50.cloned.1.call-start = ((), (), s32[]{:S(2)}) async-start(), calls=%async_computation.33 | async-start | bytes 565248
  1359.8 802.0 %reduce-scatter.52.cloned.1.call-start = ((), (), s32[]{:S(2)}) async-start(), calls=%async_computation.34 | async-start | bytes 565248
  1425.9 755.1 %reduce-scatter.36.cloned.1.call-start = ((), (), s32[]{:S(2)}) async-start(), calls=%async_computation.26 | async-start | bytes 1032192 | tf_op jit(solution)/shard_map/reduce_scatter | solution.py:337
  1648.1 552.0 %reduce-scatter.40.cloned.1.call-start = ((), (), s32[]{:S(2)}) async-start(), calls=%async_computation.28 | async-start | bytes 1032192 | tf_op jit(solution)/shard_map/reduce_scatter | solution.py:340
  1869.9 348.9 %reduce-scatter.44.cloned.1.call-start = ((), (), s32[]{:S(2)}) async-start(), calls=%async_computation.30 | async-start | bytes 1032192 | tf_op jit(solution)/shard_map/reduce_scatter | solution.py:343
  (315 other events, 2308.9 us)
Sparse Core Ops, SparseCore 0:
  9.6 37.1 all-gather.7
  48.3 34.4 all-gather.9
  84.3 34.4 all-gather.11
  120.2 34.4 all-gather.13
  156.1 133.3 all-gather.15
  291.0 131.7 all-gather.17
  1162.3 63.3 reduce-scatter.25
  1229.9 62.0 reduce-scatter.27
  1295.8 62.0 reduce-scatter.29
  1362.0 61.9 reduce-scatter.31
  1428.2 217.5 reduce-scatter.33
  1649.9 217.6 reduce-scatter.37
  1871.8 217.6 reduce-scatter.41
  2092.1 8.8 reduce-scatter.53
  2103.6 12.9 reduce-scatter.45
  2118.7 12.9 reduce-scatter.47
  2133.8 12.9 reduce-scatter.49
  2148.8 12.9 reduce-scatter.51
  2164.6 16.3 reduce-scatter.35
  2183.7 16.3 reduce-scatter.39
  2202.4 16.3 reduce-scatter.43
